TPU v7x, 32 devices: a whole 2x2x4 slice. The times are simulated.
32 devices in a mesh: order: 4 (over z), degree: 2 (over y), site: 4 (over x, core).
Axes of the slice: x: 2, y: 2, z: 4, core: 2. Of those that a mesh axis runs over, the one named last changes fastest.
Arguments:
- scene_coeffs: bfloat16 [2, 16, 128, 256, 32], P(None, None, 'degree', 'order'), may hold values from -3 to 3
- site_ids: int32 [4], P('site'), may hold values from 0 to 31
- gripper_coeffs: bfloat16 [2, 16, 128, 256], P(None, None, 'degree', 'order'), may hold values from -3 to 3
- order_table: int32 [256], replicated, may hold values from 0 to 255, each once
- wigner: bfloat16 [128, 8, 256, 256], P('degree', None, 'order'), may hold values from -0.0029907227 to 0.0029907227
Outputs:
- scores: float32 [4, 8, 256, 256], P('site', 'degree', 'order')
Inputs may be any that keep to these rules, and one draw needn't show every extreme that they name: A permutation of the 256 slots; slot j holds order order_table[j] - 128. `site_ids`: sites may share a candidate.
All inputs are finite; a program needn't handle non-finite values.
Results may differ from a plain program's by a relative error of at most 0.0029.
Values may be sent and summed in bfloat16 or wider, within the bound.
A program may use at most 128 MiB of HBM per device.

v0:
```python
import math

import jax
import jax.numpy as jnp
from jax import lax
from jax.experimental import pallas as pl
from jax.experimental.pallas import tpu as pltpu
from jax.sharding import PartitionSpec as P


def general_shards(scene_coeffs, site_ids, gripper_coeffs, order_table, wigner):
    highest = lax.Precision.HIGHEST
    slot_count = order_table.shape[0]
    local_deg = gripper_coeffs.shape[2]
    local_ord = gripper_coeffs.shape[3]
    cand_count = scene_coeffs.shape[4]
    site_count = site_ids.shape[0]
    order_pos = lax.axis_index("order")
    degree_pos = lax.axis_index("degree")
    orders = order_table - slot_count // 2
    angles = jnp.arange(slot_count, dtype=jnp.int32)
    phase_index = jnp.mod(orders[:, None] * angles[None, :], slot_count)
    radians = phase_index.astype(jnp.float32) * (2.0 * math.pi / slot_count)
    cosine = jnp.cos(radians)
    sine_table = jnp.sin(radians)
    magnitude = jnp.abs(orders)
    resident_degrees = degree_pos * local_deg + jnp.arange(local_deg, dtype=jnp.int32)
    owned_orders = lax.dynamic_slice_in_dim(magnitude, order_pos * local_ord, local_ord)
    grip_allowed = owned_orders[None, :] <= resident_degrees[:, None]
    selector = (jnp.arange(cand_count, dtype=jnp.int32)[:, None] == site_ids[None, :]).astype(
        jnp.bfloat16
    )
    chosen = jnp.dot(
        scene_coeffs.reshape(-1, cand_count), selector, preferred_element_type=jnp.float32
    )
    chosen = chosen.astype(jnp.bfloat16).reshape(
        2, scene_coeffs.shape[1], local_deg, local_ord, site_count
    )
    grip_real = jnp.concatenate([gripper_coeffs[0], gripper_coeffs[1]], axis=0)
    grip_imag = jnp.concatenate([-gripper_coeffs[1], gripper_coeffs[0]], axis=0)
    gripper_couple = jnp.stack([grip_real, grip_imag])
    columns_in = lax.all_gather(chosen, "order", axis=3, tiled=True)
    scene_joined = jnp.concatenate([columns_in[0], columns_in[1]], axis=0)
    product = jnp.einsum(
        "aonw,iaob->iobnw", scene_joined, gripper_couple, preferred_element_type=jnp.float32
    )
    permitted_mask = grip_allowed[:, :, None] & (
        magnitude[None, None, :] <= resident_degrees[:, None, None]
    )
    product = jnp.where(permitted_mask[None, :, :, :, None], product, jnp.float32(0.0)).astype(
        jnp.bfloat16
    )
    partial_value = jnp.einsum(
        "ylprs,lbpr->ysbpr", product, wigner, preferred_element_type=jnp.float32
    )
    summed = lax.psum_scatter(partial_value, "degree", scatter_dimension=2, tiled=True)
    phase_pair = jnp.concatenate([cosine, sine_table], axis=1)
    products = jnp.einsum(
        "xsbpm,mk->xsbpk", summed, phase_pair, precision=highest, preferred_element_type=jnp.float32
    )
    real_alpha = products[0, ..., :slot_count] - products[1, ..., slot_count:]
    imag_alpha = products[0, ..., slot_count:] + products[1, ..., :slot_count]
    stacked_parts = jnp.stack([real_alpha, imag_alpha])
    exchanged = lax.all_to_all(stacked_parts, "order", split_axis=4, concat_axis=3, tiled=True)
    first_term = jnp.einsum(
        "sbpa,pk->sbak", exchanged[0], cosine, precision=highest, preferred_element_type=jnp.float32
    )
    latter_addend = jnp.einsum(
        "sbpa,pk->sbak",
        exchanged[1],
        sine_table,
        precision=highest,
        preferred_element_type=jnp.float32,
    )
    return first_term - latter_addend


MESH = pl.DeviceIdType.MESH
F32, BF16 = jnp.float32, jnp.bfloat16
CHUNKS = 4
ROWS = 16


def cos_of(index, count):
    centred = jnp.bitwise_and(index + count // 2, count - 1) - count // 2
    half = centred.astype(F32) * F32(math.pi / count)
    sq = half * half
    poly = F32(-1.0 / 39916800.0)
    for coefficient in (1.0 / 362880.0, -1.0 / 5040.0, 1.0 / 120.0, -1.0 / 6.0, 1.0):
        poly = poly * sq + F32(coefficient)
    sine = poly * half
    return 1.0 - 2.0 * sine * sine


def split(value):
    high = value.astype(BF16)
    return high, (value - high.astype(F32)).astype(BF16)


def fused_kernel(
    s_ref, g_ref, row_ref, w_ref, out_ref,
    wbuf, sbuf, prod, accbuf, rs_send, rs_recv, a_send, a_recv, halfacc,
    alpha_hi, alpha_lo, gamma_hi, gamma_lo, g32, col,
    w_sem, s_send_sem, s_recv_sem, r_send_sem, r_recv_sem, x_send_sem, x_recv_sem,
):
    me = lax.axis_index("order")
    deg = lax.axis_index("degree")
    HL, NBETA, P, M = wbuf.shape[2:]
    L = 2 * HL
    SL = 2 * M
    BO = NBETA // 2
    K = s_ref.shape[1]
    first = me // 2
    second = 1 - first
    near = first * 2 + (1 - me % 2)
    per = HL // CHUNKS
    blocks = P // ROWS

    def w_copy(h, c):
        return pltpu.make_async_copy(
            w_ref.at[:, pl.ds(c * per, per), :, :, pl.ds(pl.multiple_of(h * M, M), M)],
            wbuf.at[h, :, pl.ds(c * per, per)],
            w_sem.at[h, c],
        )

    barrier = pltpu.get_barrier_semaphore()
    for off in (1, 2, 3):
        pl.semaphore_signal(barrier, 1, device_id={"order": (me + off) % 4}, device_id_type=MESH)
    pl.semaphore_signal(barrier, 1, device_id={"degree": 1 - deg}, device_id_type=MESH)

    for h in (first, second):
        for c in range(CHUNKS):
            w_copy(h, c).start()

    pl.semaphore_wait(barrier, 4)

    def hop(block, c, way, own=False):
        rows = pl.ds(c * per, per)
        return pltpu.make_async_remote_copy(
            src_ref=s_ref.at[rows] if own else sbuf.at[block, rows],
            dst_ref=sbuf.at[block, rows],
            send_sem=s_send_sem.at[way, block, c], recv_sem=s_recv_sem.at[block, c],
            device_id={"order": me + 1 - 2 * way}, device_id_type=MESH,
        )

    for c in range(CHUNKS):
        @pl.when(me < 3)
        def _():
            hop(me, c, 0, True).start()

        @pl.when(me > 0)
        def _():
            hop(me, c, 1, True).start()

    sbuf[me] = s_ref[...]

    for h in range(2):
        line = jnp.broadcast_to(row_ref[h].astype(F32), (M, M))
        col[h * M : (h + 1) * M, :] = jnp.transpose(line).astype(jnp.int32) - SL // 2
    real = g_ref[0].astype(F32).reshape(K // 2 * L, P)
    imag = g_ref[1].astype(F32).reshape(K // 2 * L, P)
    g32[: K // 2 * L] = jnp.concatenate([real, -imag], axis=1)
    g32[K // 2 * L :] = jnp.concatenate([imag, real], axis=1)
    accbuf[...] = jnp.zeros_like(accbuf)
    mag_p = jnp.abs(col[pl.ds(pl.multiple_of(me * P, P), P), :])
    dims = (((0,), (0,)), ((), ()))

    def tables():
        quarter = SL // 4
        lane = lax.broadcasted_iota(jnp.int32, (M, M), 1)
        for h in range(2):
            orders = col[h * M : (h + 1) * M, :]
            for t in range(4):
                at = slice(t * M, (t + 1) * M)
                phase = orders * (t * P + lane % P)
                for x in range(2):
                    hi, lo = split(cos_of(phase + (x - lane // P) * quarter, SL))
                    alpha_hi[h, x * M : (x + 1) * M, at] = hi
                    alpha_lo[h, x * M : (x + 1) * M, at] = lo
                phase = orders * ((t % 2) * M + lane)
                hi, lo = split(cos_of(phase + (t // 2) * quarter, SL))
                gamma_hi[h * M : (h + 1) * M, at] = hi
                gamma_lo[h * M : (h + 1) * M, at] = lo

    def r_copy(h, blk):
        return pltpu.make_async_remote_copy(
            src_ref=rs_send.at[h, blk], dst_ref=rs_recv.at[h, blk],
            send_sem=r_send_sem.at[h, blk], recv_sem=r_recv_sem.at[h, blk],
            device_id={"degree": 1 - deg}, device_id_type=MESH,
        )

    def compute(h, arrivals):
        mag_m = jnp.abs(row_ref[h] - SL // 2)
        most = jnp.maximum(mag_p, jnp.broadcast_to(mag_m, (P, M)))
        most = jnp.concatenate([most, most], axis=0)

        def chunk(c, carry):
            arrivals(c)
            for i in range(per):
                step = c * per + i
                b0, b1 = sbuf[2 * h, step], sbuf[2 * h + 1, step]
                low = jnp.concatenate([b0[:, :P], b1[:, :P]], axis=1)
                high = jnp.concatenate([b0[:, P:], b1[:, P:]], axis=1)
                for part, scene in ((0, low), (1, high)):
                    l = step + part * HL
                    grip = g32[pl.ds(l, K, stride=L), :].astype(BF16)
                    value = lax.dot_general(grip, scene, dims, preferred_element_type=F32)
                    value = jnp.where(most <= deg * L + l, value, F32(0.0))
                    prod[part, i] = value.astype(BF16)
            w_copy(h, c).wait()

            def rows(blk, carry):
                at = pl.multiple_of(blk * ROWS, ROWS)

                def degree_step(i, acc):
                    acc = list(acc)
                    for part in range(2):
                        pr = prod[part, i, pl.ds(at, ROWS), :].astype(F32)
                        pi = prod[part, i, pl.ds(at + P, ROWS), :].astype(F32)
                        for b in range(NBETA):
                            w = wbuf[h, part, c * per + i, b, pl.ds(at, ROWS), :].astype(F32)
                            acc[2 * b] += pr * w
                            acc[2 * b + 1] += pi * w
                    return tuple(acc)

                acc = tuple(accbuf[h, blk, n // 2, n % 2] for n in range(2 * NBETA))
                acc = lax.fori_loop(0, per, degree_step, acc, unroll=2)
                for n in range(2 * NBETA):
                    accbuf[h, blk, n // 2, n % 2] = acc[n]

                @pl.when(c == CHUNKS - 1)
                def _():
                    rs_send[h, blk] = accbuf[h, blk, pl.ds((1 - deg) * BO, BO)].astype(BF16)
                    r_copy(h, blk).start()

                return carry

            return lax.fori_loop(0, blocks, rows, carry)

        lax.fori_loop(0, CHUNKS, chunk, 0)

    def alpha(h, blk):
        r_copy(h, blk).wait_recv()
        total = accbuf[h, blk, pl.ds(deg * BO, BO)] + rs_recv[h, blk].astype(F32)
        total = jnp.concatenate(
            [total[:, 0].reshape(BO * ROWS, M), total[:, 1].reshape(BO * ROWS, M)], axis=1
        )
        hi, lo = split(total)
        value = jnp.dot(hi, alpha_hi[h], preferred_element_type=F32)
        value += jnp.dot(hi, alpha_lo[h], preferred_element_type=F32)
        value += jnp.dot(lo, alpha_hi[h], preferred_element_type=F32)
        return value

    across = lax.max(me - 1, 0) % 2
    middle = (me == 1) | (me == 2)
    other = me + 1 - 2 * across
    beyond = other + 1 - 2 * across

    def wait_block(block, c):
        hop(block, c, me // 3).wait_recv()

    def arrivals_first(c):
        wait_block(near, c)

        @pl.when(middle)
        def _():
            hop(near, c, across).start()
            wait_block(other, c)
            hop(other, c, 1 - across).start()

    def arrivals_second(c):
        @pl.when(middle)
        def _():
            wait_block(beyond, c)
            hop(beyond, c, 1 - across).start()

        @pl.when(jnp.logical_not(middle))
        def _():
            wait_block(second * 2, c)
            wait_block(second * 2 + 1, c)

    tables()
    compute(first, arrivals_first)
    compute(second, arrivals_second)

    def x_copy(target, source, blk, off):
        return pltpu.make_async_remote_copy(
            src_ref=a_send.at[target, blk], dst_ref=a_recv.at[source, blk],
            send_sem=x_send_sem.at[off, blk], recv_sem=x_recv_sem.at[off, blk],
            device_id={"order": target}, device_id_type=MESH,
        )

    for blk in range(blocks):
        halfacc[blk] = alpha(first, blk)
    for blk in range(blocks):
        value = (halfacc[blk] + alpha(second, blk)).astype(BF16)
        for t in range(4):
            a_send[t, blk] = value[:, t * M : (t + 1) * M]
        for off in (2, 1, 3):
            x_copy((me + off) % 4, me, blk, off).start()
        a_recv[me, blk] = a_send[me, blk]

    for blk in range(blocks):
        for off in (1, 3, 2):
            source = (me - off + 4) % 4
            x_copy(source, source, blk, off).wait_recv()

    score = jnp.zeros((BO * P, SL), F32)
    got = [
        jnp.concatenate(
            [a_recv[z, blk, b * ROWS : (b + 1) * ROWS, :] for z in range(4) for blk in range(blocks)],
            axis=0,
        )
        for b in range(BO)
    ]
    for x in range(2):
        left = jnp.concatenate([piece[:, x * P : (x + 1) * P] for piece in got], axis=1)
        for table in (gamma_hi, gamma_lo):
            score += lax.dot_general(
                left, table[:, x * SL : (x + 1) * SL], dims, preferred_element_type=F32
            )
    out_ref[0] = score.reshape(BO, P, SL)

    for c in range(CHUNKS):
        @pl.when(me < 3)
        def _():
            hop(me, c, 0, True).wait_send()

        @pl.when(me > 0)
        def _():
            hop(me, c, 1, True).wait_send()

        @pl.when(middle)
        def _():
            hop(near, c, across).wait_send()
            hop(other, c, 1 - across).wait_send()
            hop(beyond, c, 1 - across).wait_send()

    for blk in range(blocks):
        for off in (1, 2, 3):
            x_copy((me + off) % 4, me, blk, off).wait_send()
        r_copy(first, blk).wait_send()
        r_copy(second, blk).wait_send()


def fused_shards(scene_coeffs, site_ids, gripper_coeffs, order_table, wigner):
    L, NBETA, P, SL = wigner.shape
    M = SL // 2
    K = 2 * scene_coeffs.shape[1]
    BO = NBETA // 2
    NB = P // ROWS
    chosen = lax.dynamic_index_in_dim(scene_coeffs, site_ids[0], axis=4, keepdims=False)
    s = jnp.transpose(chosen, (2, 0, 1, 3)).reshape(2, L // 2, K, P)
    s = jnp.concatenate([s[0], s[1]], axis=-1)
    vmem = pl.BlockSpec(memory_space=pltpu.VMEM)
    return pl.pallas_call(
        fused_kernel,
        out_shape=jax.ShapeDtypeStruct((1, BO, P, SL), F32),
        in_specs=[vmem, vmem, vmem, pl.BlockSpec(memory_space=pl.ANY)],
        out_specs=vmem,
        scratch_shapes=[
            pltpu.VMEM((2, 2, L // 2, NBETA, P, M), BF16),
            pltpu.VMEM((4, L // 2, K, 2 * P), BF16),
            pltpu.VMEM((2, L // 2 // CHUNKS, 2 * P, M), BF16),
            pltpu.VMEM((2, NB, NBETA, 2, ROWS, M), F32),
            pltpu.VMEM((2, NB, BO, 2, ROWS, M), BF16),
            pltpu.VMEM((2, NB, BO, 2, ROWS, M), BF16),
            pltpu.VMEM((4, NB, BO * ROWS, M), BF16),
            pltpu.VMEM((4, NB, BO * ROWS, M), BF16),
            pltpu.VMEM((NB, BO * ROWS, 2 * SL), F32),
            pltpu.VMEM((2, 2 * M, 2 * SL), BF16),
            pltpu.VMEM((2, 2 * M, 2 * SL), BF16),
            pltpu.VMEM((SL, 2 * SL), BF16),
            pltpu.VMEM((SL, 2 * SL), BF16),
            pltpu.VMEM((K * L, 2 * P), F32),
            pltpu.VMEM((SL, M), jnp.int32),
            pltpu.SemaphoreType.DMA((2, CHUNKS)),
            pltpu.SemaphoreType.DMA((2, 4, CHUNKS)),
            pltpu.SemaphoreType.DMA((4, CHUNKS)),
            pltpu.SemaphoreType.DMA((2, NB)),
            pltpu.SemaphoreType.DMA((2, NB)),
            pltpu.SemaphoreType.DMA((4, NB)),
            pltpu.SemaphoreType.DMA((4, NB)),
        ],
        compiler_params=pltpu.CompilerParams(
            collective_id=0, has_side_effects=True, vmem_limit_bytes=48 * 1024 * 1024
        ),
    )(s, gripper_coeffs, order_table.reshape(2, 1, M), wigner.reshape(2, L // 2, NBETA, P, SL))


def solution(mesh):
    fits = mesh.shape["order"] == 4 and mesh.shape["degree"] == 2 and mesh.shape["site"] == 4
    shards = fused_shards if fits else general_shards
    in_specs = (
        P(None, None, "degree", "order", None),
        P("site"),
        P(None, None, "degree", "order"),
        P(),
        P("degree", None, "order", None),
    )
    out_specs = P("site", "degree", "order", None)
    return jax.shard_map(shards, mesh=mesh, in_specs=in_specs, out_specs=out_specs, check_vma=False)
```

profile of v0, /device:TPU:0, one launch (start us, length us, event | category | flops | bytes accessed | tf_op | source)
XLA Modules:
  0.0 42.1 jit_solution(8391144225670339985)
XLA Ops:
  0.7 3.5 %constant_dynamic-slice_fusion = bf16[2,16,64,64,1]{3,4,2,1,0:T(2,128)(2,1)S(1)} fusion(bf16[2,16,64,64,32]{3,4,2,1,0:T(8,128)(2,1)} %param.5, s32[]{:T(128)S(6)} %select_n.4), kind=kLoop, calls=%fused_computation.2 | loop fusion | bytes 524292 | tf_op jit(solution)/shard_map/jit(dynamic_index_in_dim)/dynamic_slice | solution.py:352
  4.2 0.1 copy.11
  4.3 0.1 copy.7
  4.4 0.1 copy.8
  4.5 0.1 pad_maximum_fusion.s_ref
  4.7 0.0 copy-start
  4.7 1.0 %copy-done = bf16[2,16,64,64]{3,2,1,0:T(8,128)(2,1)S(1)} copy-done((bf16[2,16,64,64]{3,2,1,0:T(8,128)(2,1)S(1)}, bf16[2,16,64,64]{3,2,1,0:T(8,128)(2,1)}, u32[]{:S(2)}) %copy-start) | copy-done | bytes 262168
  5.7 0.0 copy-start.1
  5.7 0.7 %copy-done.1 = s32[256]{0:T(256)S(1)} copy-done((s32[256]{0:T(256)S(1)}, s32[256]{0:T(256)}, u32[]{:S(2)}) %copy-start.1) | copy-done | bytes 1048
  6.4 35.0 %shard_map.55 = f32[1,4,64,256]{3,2,1,0:T(8,128)S(1)} custom-call(bf16[32,32,128]{2,1,0:T(8,128)(2,1)S(1)} %pad_maximum_fusion.s_ref, bf16[2,16,64,64]{3,2,1,0:T(8,128)(2,1)S(1)} %copy-done, s32[2,1,128]{2,1,0:T(1,128)S(1)} %bitcast.13, bf16[2,32,8,64,256]{4,3,2,1,0:T(8,128)(2,1)} %bitcast.14), custom_call_target="tpu_custom_call" | custom-call | tf_op jit(solution)/shard_map/pallas_call | solution.py:356
  41.4 0.7 %copy.14 = f32[1,4,64,256]{3,2,1,0:T(8,128)} copy(f32[1,4,64,256]{3,2,1,0:T(8,128)S(1)} %shard_map.55) | data formatting | bytes 524288
  (1 shorter events, 0.0 us)
Async XLA Ops:
  4.7 1.0 %copy-start = (bf16[2,16,64,64]{3,2,1,0:T(8,128)(2,1)S(1)}, bf16[2,16,64,64]{3,2,1,0:T(8,128)(2,1)}, u32[]{:S(2)}) copy-start(bf16[2,16,64,64]{3,2,1,0:T(8,128)(2,1)} %g_ref.1) | copy-start | bytes 786436
  5.7 0.7 %copy-start.1 = (s32[256]{0:T(256)S(1)}, s32[256]{0:T(256)}, u32[]{:S(2)}) copy-start(s32[256]{0:T(256)} %param.8) | copy-start | bytes 3076
where the time goes:
time: 42.3 us; the launch traced here: 42.1 us
  Pallas kernels  35 us (83%)
  local copies, waits for them, and re-layouts  6.25 us (15%)
  between operations  0.72 us (2%)
    pallas_call x1, Pallas kernels, fused_shards(): pl.pallas_call(fused_kernel, out_shape=jax.ShapeDtypeStruct((1, BO, P, SL...  35 us
    dynamic_slice x1, local copies, waits for them, and re-layouts, fused_shards(): lax.dynamic_index_in_dim(scene_coeffs, site_ids[0], axis=4, keepdims=False)  3.51 us
    unnamed x6, local copies, waits for them, and re-layouts  2.5 us

commit v1 on v0

--- a/solution.py
+++ b/solution.py
@@ -79,6 +79,7 @@
 F32, BF16 = jnp.float32, jnp.bfloat16
 CHUNKS = 4
 ROWS = 16
+GROUP = 8
 
 
 def cos_of(index, count):
@@ -98,10 +99,17 @@
 
 
 def fused_kernel(
-    s_ref, g_ref, row_ref, w_ref, out_ref,
-    wbuf, sbuf, prod, accbuf, rs_send, rs_recv, a_send, a_recv, halfacc,
+    scene_ref, site_ref, g_hbm, row_hbm, w_ref, out_ref, wbuf, *scratch
+):
+    cands, scratch = scratch[:CHUNKS], scratch[CHUNKS:]
+    fused_body(scene_ref, site_ref, g_hbm, row_hbm, w_ref, out_ref, wbuf, cands, *scratch)
+
+
+def fused_body(
+    scene_ref, site_ref, g_hbm, row_hbm, w_ref, out_ref, wbuf, cands,
+    g_ref, row_ref, sbuf, prod, accbuf, rs_send, rs_recv, a_send, a_recv, halfacc,
     alpha_hi, alpha_lo, gamma_hi, gamma_lo, g32, col,
-    w_sem, s_send_sem, s_recv_sem, r_send_sem, r_recv_sem, x_send_sem, x_recv_sem,
+    in_sem, c_sem, w_sem, s_send_sem, s_recv_sem, r_send_sem, r_recv_sem, x_send_sem, x_recv_sem,
 ):
     me = lax.axis_index("order")
     deg = lax.axis_index("degree")
@@ -109,7 +117,7 @@
     L = 2 * HL
     SL = 2 * M
     BO = NBETA // 2
-    K = s_ref.shape[1]
+    K = scene_ref.shape[0]
     first = me // 2
     second = 1 - first
     near = first * 2 + (1 - me % 2)
@@ -123,46 +131,72 @@
             w_sem.at[h, c],
         )
 
+    def c_copy(c):
+        return pltpu.make_async_copy(
+            scene_ref.at[:, :, pl.ds(c * per, per)], cands[c], c_sem.at[c]
+        )
+
+    c_copy(0).start()
+    g_copy = pltpu.make_async_copy(g_hbm, g_ref, in_sem.at[0])
+    row_copy = pltpu.make_async_copy(row_hbm, row_ref, in_sem.at[1])
+    row_copy.start()
+    g_copy.start()
+    for c in range(1, CHUNKS):
+        c_copy(c).start()
+
     barrier = pltpu.get_barrier_semaphore()
     for off in (1, 2, 3):
         pl.semaphore_signal(barrier, 1, device_id={"order": (me + off) % 4}, device_id_type=MESH)
     pl.semaphore_signal(barrier, 1, device_id={"degree": 1 - deg}, device_id_type=MESH)
 
-    for h in (first, second):
-        for c in range(CHUNKS):
-            w_copy(h, c).start()
-
-    pl.semaphore_wait(barrier, 4)
-
-    def hop(block, c, way, own=False):
+    site = site_ref[0]
+    pick_row = lax.broadcasted_iota(jnp.int32, (K, K * GROUP), 0)
+    pick_col = lax.broadcasted_iota(jnp.int32, (K, K * GROUP), 1)
+    pick = (pick_col == pick_row * GROUP + site % GROUP).astype(F32).astype(BF16)
+
+    def select(c):
+        def step(i, carry):
+            halves = []
+            for part in range(2):
+                tile = cands[c][:, part, i, site // GROUP].astype(F32)
+                tile = tile.reshape(K * GROUP, P).astype(BF16)
+                halves.append(jnp.dot(pick, tile, preferred_element_type=F32))
+            sbuf[me, c * per + i] = jnp.concatenate(halves, axis=1).astype(BF16)
+            return carry
+
+        c_copy(c).wait()
+        lax.fori_loop(0, per, step, 0, unroll=True)
+
+    def hop(block, c, way):
         rows = pl.ds(c * per, per)
         return pltpu.make_async_remote_copy(
-            src_ref=s_ref.at[rows] if own else sbuf.at[block, rows],
+            src_ref=sbuf.at[block, rows],
             dst_ref=sbuf.at[block, rows],
             send_sem=s_send_sem.at[way, block, c], recv_sem=s_recv_sem.at[block, c],
             device_id={"order": me + 1 - 2 * way}, device_id_type=MESH,
         )
 
-    for c in range(CHUNKS):
+    def send_own(c):
         @pl.when(me < 3)
         def _():
-            hop(me, c, 0, True).start()
+            hop(me, c, 0).start()
 
         @pl.when(me > 0)
         def _():
-            hop(me, c, 1, True).start()
-
-    sbuf[me] = s_ref[...]
-
-    for h in range(2):
-        line = jnp.broadcast_to(row_ref[h].astype(F32), (M, M))
-        col[h * M : (h + 1) * M, :] = jnp.transpose(line).astype(jnp.int32) - SL // 2
-    real = g_ref[0].astype(F32).reshape(K // 2 * L, P)
-    imag = g_ref[1].astype(F32).reshape(K // 2 * L, P)
-    g32[: K // 2 * L] = jnp.concatenate([real, -imag], axis=1)
-    g32[K // 2 * L :] = jnp.concatenate([imag, real], axis=1)
-    accbuf[...] = jnp.zeros_like(accbuf)
-    mag_p = jnp.abs(col[pl.ds(pl.multiple_of(me * P, P), P), :])
+            hop(me, c, 1).start()
+
+    def prepare():
+        row_copy.wait()
+        for h in range(2):
+            line = jnp.broadcast_to(row_ref[h].astype(F32), (M, M))
+            col[h * M : (h + 1) * M, :] = jnp.transpose(line).astype(jnp.int32) - SL // 2
+        g_copy.wait()
+        real = g_ref[0].astype(F32).reshape(K // 2 * L, P)
+        imag = g_ref[1].astype(F32).reshape(K // 2 * L, P)
+        g32[: K // 2 * L] = jnp.concatenate([real, -imag], axis=1)
+        g32[K // 2 * L :] = jnp.concatenate([imag, real], axis=1)
+        accbuf[...] = jnp.zeros_like(accbuf)
+
     dims = (((0,), (0,)), ((), ()))
 
     def tables():
@@ -190,6 +224,7 @@
         )
 
     def compute(h, arrivals):
+        mag_p = jnp.abs(col[pl.ds(pl.multiple_of(me * P, P), P), :])
         mag_m = jnp.abs(row_ref[h] - SL // 2)
         most = jnp.maximum(mag_p, jnp.broadcast_to(mag_m, (P, M)))
         most = jnp.concatenate([most, most], axis=0)
@@ -279,8 +314,25 @@
             wait_block(second * 2, c)
             wait_block(second * 2 + 1, c)
 
+    select(0)
+    pl.semaphore_wait(barrier, 4)
+    send_own(0)
+    select(1)
+    send_own(1)
+    w_copy(first, 0).start()
+    for c in range(2, CHUNKS):
+        arrivals_first(c - 2)
+        select(c)
+        send_own(c)
+        w_copy(first, c - 1).start()
+    w_copy(first, CHUNKS - 1).start()
+    for c in range(CHUNKS):
+        w_copy(second, c).start()
+    arrivals_first(CHUNKS - 2)
+    prepare()
+    arrivals_first(CHUNKS - 1)
     tables()
-    compute(first, arrivals_first)
+    compute(first, lambda c: None)
     compute(second, arrivals_second)
 
     def x_copy(target, source, blk, off):
@@ -324,11 +376,11 @@
     for c in range(CHUNKS):
         @pl.when(me < 3)
         def _():
-            hop(me, c, 0, True).wait_send()
+            hop(me, c, 0).wait_send()
 
         @pl.when(me > 0)
         def _():
-            hop(me, c, 1, True).wait_send()
+            hop(me, c, 1).wait_send()
 
         @pl.when(middle)
         def _():
@@ -349,17 +401,24 @@
     K = 2 * scene_coeffs.shape[1]
     BO = NBETA // 2
     NB = P // ROWS
-    chosen = lax.dynamic_index_in_dim(scene_coeffs, site_ids[0], axis=4, keepdims=False)
-    s = jnp.transpose(chosen, (2, 0, 1, 3)).reshape(2, L // 2, K, P)
-    s = jnp.concatenate([s[0], s[1]], axis=-1)
+    cand = scene_coeffs.shape[4]
+    tall = jnp.transpose(scene_coeffs, (0, 1, 2, 4, 3))
+    tall = tall.reshape(K, 2, L // 2, cand // GROUP, GROUP, P)
     vmem = pl.BlockSpec(memory_space=pltpu.VMEM)
+    hbm = pl.BlockSpec(memory_space=pltpu.HBM)
     return pl.pallas_call(
         fused_kernel,
         out_shape=jax.ShapeDtypeStruct((1, BO, P, SL), F32),
-        in_specs=[vmem, vmem, vmem, pl.BlockSpec(memory_space=pl.ANY)],
+        in_specs=[hbm, pl.BlockSpec(memory_space=pltpu.SMEM), hbm, hbm, hbm],
         out_specs=vmem,
         scratch_shapes=[
             pltpu.VMEM((2, 2, L // 2, NBETA, P, M), BF16),
+            *[
+                pltpu.VMEM((K, 2, L // 2 // CHUNKS, cand // GROUP, GROUP, P), BF16)
+                for _ in range(CHUNKS)
+            ],
+            pltpu.VMEM((2, K // 2, L, P), BF16),
+            pltpu.VMEM((2, 1, M), jnp.int32),
             pltpu.VMEM((4, L // 2, K, 2 * P), BF16),
             pltpu.VMEM((2, L // 2 // CHUNKS, 2 * P, M), BF16),
             pltpu.VMEM((2, NB, NBETA, 2, ROWS, M), F32),
@@ -374,6 +433,8 @@
             pltpu.VMEM((SL, 2 * SL), BF16),
             pltpu.VMEM((K * L, 2 * P), F32),
             pltpu.VMEM((SL, M), jnp.int32),
+            pltpu.SemaphoreType.DMA((2,)),
+            pltpu.SemaphoreType.DMA((CHUNKS,)),
             pltpu.SemaphoreType.DMA((2, CHUNKS)),
             pltpu.SemaphoreType.DMA((2, 4, CHUNKS)),
             pltpu.SemaphoreType.DMA((4, CHUNKS)),
@@ -385,7 +446,13 @@
         compiler_params=pltpu.CompilerParams(
             collective_id=0, has_side_effects=True, vmem_limit_bytes=48 * 1024 * 1024
         ),
-    )(s, gripper_coeffs, order_table.reshape(2, 1, M), wigner.reshape(2, L // 2, NBETA, P, SL))
+    )(
+        tall,
+        site_ids,
+        gripper_coeffs,
+        order_table.reshape(2, 1, M),
+        wigner.reshape(2, L // 2, NBETA, P, SL),
+    )
 
 
 def solution(mesh):

time: 42.3 us -> 46.2 us (1.092)
  Pallas kernels: 35 us -> 42.9 us
  local copies, waits for them, and re-layouts: 6.25 us -> 2.42 us
    pallas_call x1, Pallas kernels: 35 us -> 42.9 us  [fused_shards(): pl.pallas_call(fused_kernel, out_shape=jax.ShapeDtypeStruct((1, BO, P, SL...]
    dynamic_slice x1 -> x0, local copies, waits for them, and re-layouts: 3.51 us -> none  [fused_shards(): lax.dynamic_index_in_dim(scene_coeffs, site_ids[0], axis=4, keepdims=False)]
    unnamed x6 -> x5, local copies, waits for them, and re-layouts: 2.5 us -> 2.42 us
where the time goes in v1:
time: 46.2 us; the launch traced here: 46 us
  Pallas kernels  42.9 us (93%)
  local copies, waits for them, and re-layouts  2.42 us (5%)
  between operations  0.67 us (1%)
    pallas_call x1, Pallas kernels, fused_shards(): pl.pallas_call(fused_kernel, out_shape=jax.ShapeDtypeStruct((1, BO, P, SL...  42.9 us
    unnamed x5, local copies, waits for them, and re-layouts  2.42 us

profile of v1, /device:TPU:0, one launch (start us, length us, event | category | flops | bytes accessed | tf_op | source)
XLA Modules:
  0.0 46.0 jit_solution(15650377233237424175)
XLA Ops:
  0.7 0.0 copy-start
  0.7 1.0 %copy-done = bf16[2,16,64,64]{3,2,1,0:T(8,128)(2,1)S(1)} copy-done((bf16[2,16,64,64]{3,2,1,0:T(8,128)(2,1)S(1)}, bf16[2,16,64,64]{3,2,1,0:T(8,128)(2,1)}, u32[]{:S(2)}) %copy-start) | copy-done | bytes 262168
  1.7 0.0 copy-start.1
  1.7 0.7 %copy-done.1 = s32[256]{0:T(256)S(1)} copy-done((s32[256]{0:T(256)S(1)}, s32[256]{0:T(256)}, u32[]{:S(2)}) %copy-start.1) | copy-done | bytes 1048
  2.4 42.9 %shard_map.55 = f32[1,4,64,256]{3,2,1,0:T(8,128)S(1)} custom-call(bf16[32,2,32,4,8,64]{5,4,3,2,1,0:T(8,128)(2,1)} %bitcast.6, s32[1]{0:T(128)S(6)} %copy.7.site_ref, bf16[2,16,64,64]{3,2,1,0:T(8,128)(2,1)S(1)} %copy-done, s32[2,1,128]{2,1,0:T(1,128)S(1)} %bitcast.5, bf16[2,32,8,64,256]{4,3,2,1,0:T(8,128)(2,1)} %bitcast.7), custom_call_target="tpu_custom_call" | custom-call | tf_op jit(solution)/shard_map/pallas_call | solution.py:409
  45.3 0.7 %copy.8 = f32[1,4,64,256]{3,2,1,0:T(8,128)} copy(f32[1,4,64,256]{3,2,1,0:T(8,128)S(1)} %shard_map.55) | data formatting | bytes 524288
Async XLA Ops:
  0.7 1.0 %copy-start = (bf16[2,16,64,64]{3,2,1,0:T(8,128)(2,1)S(1)}, bf16[2,16,64,64]{3,2,1,0:T(8,128)(2,1)}, u32[]{:S(2)}) copy-start(bf16[2,16,64,64]{3,2,1,0:T(8,128)(2,1)} %g_hbm.1) | copy-start | bytes 786436
  1.7 0.7 %copy-start.1 = (s32[256]{0:T(256)S(1)}, s32[256]{0:T(256)}, u32[]{:S(2)}) copy-start(s32[256]{0:T(256)} %param.8) | copy-start | bytes 3076

commit v2 on v1

--- a/solution.py
+++ b/solution.py
@@ -223,14 +223,14 @@
             device_id={"degree": 1 - deg}, device_id_type=MESH,
         )
 
-    def compute(h, arrivals):
+    def compute(h, before, after):
         mag_p = jnp.abs(col[pl.ds(pl.multiple_of(me * P, P), P), :])
         mag_m = jnp.abs(row_ref[h] - SL // 2)
         most = jnp.maximum(mag_p, jnp.broadcast_to(mag_m, (P, M)))
         most = jnp.concatenate([most, most], axis=0)
 
         def chunk(c, carry):
-            arrivals(c)
+            before(c)
             for i in range(per):
                 step = c * per + i
                 b0, b1 = sbuf[2 * h, step], sbuf[2 * h + 1, step]
@@ -270,7 +270,9 @@
 
                 return carry
 
-            return lax.fori_loop(0, blocks, rows, carry)
+            lax.fori_loop(0, blocks, rows, 0)
+            after(c)
+            return carry
 
         lax.fori_loop(0, CHUNKS, chunk, 0)
 
@@ -294,7 +296,7 @@
     def wait_block(block, c):
         hop(block, c, me // 3).wait_recv()
 
-    def arrivals_first(c):
+    def collect(c):
         wait_block(near, c)
 
         @pl.when(middle)
@@ -303,16 +305,31 @@
             wait_block(other, c)
             hop(other, c, 1 - across).start()
 
-    def arrivals_second(c):
+    def relay(c):
         @pl.when(middle)
         def _():
             wait_block(beyond, c)
             hop(beyond, c, 1 - across).start()
 
+    def after_first(c):
+        @pl.when(c < CHUNKS - 2)
+        def _():
+            collect(c + 2)
+
+        @pl.when(c > 0)
+        def _():
+            relay(c - 1)
+
+    def before_second(c):
         @pl.when(jnp.logical_not(middle))
         def _():
             wait_block(second * 2, c)
             wait_block(second * 2 + 1, c)
+
+        @pl.when(c == 2)
+        def _():
+            for blk in range(blocks):
+                halfacc[blk] = alpha(first, blk)
 
     select(0)
     pl.semaphore_wait(barrier, 4)
@@ -320,20 +337,22 @@
     select(1)
     send_own(1)
     w_copy(first, 0).start()
+    select(2)
+    send_own(2)
+    w_copy(first, 1).start()
+    collect(0)
+    select(3)
+    send_own(3)
     for c in range(2, CHUNKS):
-        arrivals_first(c - 2)
-        select(c)
-        send_own(c)
-        w_copy(first, c - 1).start()
-    w_copy(first, CHUNKS - 1).start()
+        w_copy(first, c).start()
     for c in range(CHUNKS):
         w_copy(second, c).start()
-    arrivals_first(CHUNKS - 2)
+    collect(1)
     prepare()
-    arrivals_first(CHUNKS - 1)
+    compute(first, lambda c: None, after_first)
     tables()
-    compute(first, lambda c: None)
-    compute(second, arrivals_second)
+    relay(CHUNKS - 1)
+    compute(second, before_second, lambda c: None)
 
     def x_copy(target, source, blk, off):
         return pltpu.make_async_remote_copy(
@@ -342,8 +361,6 @@
             device_id={"order": target}, device_id_type=MESH,
         )
 
-    for blk in range(blocks):
-        halfacc[blk] = alpha(first, blk)
     for blk in range(blocks):
         value = (halfacc[blk] + alpha(second, blk)).astype(BF16)
         for t in range(4):
@@ -449,8 +466,8 @@
     )(
         tall,
         site_ids,
-        gripper_coeffs,
-        order_table.reshape(2, 1, M),
+        pltpu.with_memory_space_constraint(gripper_coeffs, pltpu.HBM),
+        pltpu.with_memory_space_constraint(order_table.reshape(2, 1, M), pltpu.HBM),
         wigner.reshape(2, L // 2, NBETA, P, SL),
     )
 

time: 46.2 us -> 38.4 us (0.83)
  Pallas kernels: 42.9 us -> 36.9 us
  local copies, waits for them, and re-layouts: 2.42 us -> 0.71 us
    pallas_call x1, Pallas kernels: 42.9 us -> 36.9 us  [fused_shards(): pl.pallas_call(fused_kernel, out_shape=jax.ShapeDtypeStruct((1, BO, P, SL...]
    unnamed x5 -> x1, local copies, waits for them, and re-layouts: 2.42 us -> 0.71 us
where the time goes in v2:
time: 38.4 us; the launch traced here: 38.2 us
  Pallas kernels  36.9 us (96%)
  local copies, waits for them, and re-layouts  0.71 us (2%)
  between operations  0.66 us (2%)
    pallas_call x1, Pallas kernels, fused_shards(): pl.pallas_call(fused_kernel, out_shape=jax.ShapeDtypeStruct((1, BO, P, SL...  36.9 us

profile of v2, /device:TPU:0, one launch (start us, length us, event | category | flops | bytes accessed | tf_op | source)
XLA Modules:
  0.0 38.2 jit_solution(4559772486911647052)
XLA Ops:
  0.7 36.9 %shard_map.55 = f32[1,4,64,256]{3,2,1,0:T(8,128)S(1)} custom-call(bf16[32,2,32,4,8,64]{5,4,3,2,1,0:T(8,128)(2,1)} %bitcast.5, s32[1]{0:T(128)S(6)} %copy.7.site_ref, bf16[2,16,64,64]{3,2,1,0:T(8,128)(2,1)} %g_hbm.1, s32[2,1,128]{2,1,0:T(1,128)} %bitcast.7, bf16[2,32,8,64,256]{4,3,2,1,0:T(8,128)(2,1)} %bitcast.6), custom_call_target="tpu_custom_call" | custom-call | tf_op jit(solution)/shard_map/pallas_call | solution.py:426
  37.5 0.7 %copy.8 = f32[1,4,64,256]{3,2,1,0:T(8,128)} copy(f32[1,4,64,256]{3,2,1,0:T(8,128)S(1)} %shard_map.55) | data formatting | bytes 524288

commit v3 on v1

--- a/solution.py
+++ b/solution.py
@@ -78,6 +78,18 @@
 MESH = pl.DeviceIdType.MESH
 F32, BF16 = jnp.float32, jnp.bfloat16
 CHUNKS = 4
+PIECES = (8, 8, 8, 8)
+STAGED = 4
+PLAN = (
+    "s0 s1 s2 s3",
+    "f0 f1 f2 f3",
+    "x c0 p c1",
+    "u0 c2 u1 c3",
+    "r0 u2 r1 u3",
+    "r2 t r3 v0",
+    "v1 v2 v3 a",
+)
+UNITS = ((0, 8, (0,)), (8, 8, (1,)), (16, 8, (2,)), (24, 8, (3,)))
 ROWS = 16
 GROUP = 8
 
@@ -101,7 +113,7 @@
 def fused_kernel(
     scene_ref, site_ref, g_hbm, row_hbm, w_ref, out_ref, wbuf, *scratch
 ):
-    cands, scratch = scratch[:CHUNKS], scratch[CHUNKS:]
+    cands, scratch = scratch[: len(PIECES)], scratch[len(PIECES) :]
     fused_body(scene_ref, site_ref, g_hbm, row_hbm, w_ref, out_ref, wbuf, cands, *scratch)
 
 
@@ -131,9 +143,11 @@
             w_sem.at[h, c],
         )
 
+    starts = [sum(PIECES[:i]) for i in range(len(PIECES))]
+
     def c_copy(c):
         return pltpu.make_async_copy(
-            scene_ref.at[:, :, pl.ds(c * per, per)], cands[c], c_sem.at[c]
+            scene_ref.at[:, :, pl.ds(starts[c], PIECES[c])], cands[c], c_sem.at[c]
         )
 
     c_copy(0).start()
@@ -141,7 +155,7 @@
     row_copy = pltpu.make_async_copy(row_hbm, row_ref, in_sem.at[1])
     row_copy.start()
     g_copy.start()
-    for c in range(1, CHUNKS):
+    for c in range(1, STAGED):
         c_copy(c).start()
 
     barrier = pltpu.get_barrier_semaphore()
@@ -158,17 +172,16 @@
         def step(i, carry):
             halves = []
             for part in range(2):
-                tile = cands[c][:, part, i, site // GROUP].astype(F32)
-                tile = tile.reshape(K * GROUP, P).astype(BF16)
+                tile = cands[c][:, part, i, site // GROUP].reshape(K * GROUP, P)
                 halves.append(jnp.dot(pick, tile, preferred_element_type=F32))
-            sbuf[me, c * per + i] = jnp.concatenate(halves, axis=1).astype(BF16)
+            sbuf[me, starts[c] + i] = jnp.concatenate(halves, axis=1).astype(BF16)
             return carry
 
         c_copy(c).wait()
-        lax.fori_loop(0, per, step, 0, unroll=True)
+        lax.fori_loop(0, PIECES[c], step, 0, unroll=True)
 
     def hop(block, c, way):
-        rows = pl.ds(c * per, per)
+        rows = pl.ds(starts[c], PIECES[c])
         return pltpu.make_async_remote_copy(
             src_ref=sbuf.at[block, rows],
             dst_ref=sbuf.at[block, rows],
@@ -202,17 +215,28 @@
     def tables():
         quarter = SL // 4
         lane = lax.broadcasted_iota(jnp.int32, (M, M), 1)
+        left = lane < P
         for h in range(2):
             orders = col[h * M : (h + 1) * M, :]
+            upright, turned = [], []
             for t in range(4):
                 at = slice(t * M, (t + 1) * M)
-                phase = orders * (t * P + lane % P)
-                for x in range(2):
-                    hi, lo = split(cos_of(phase + (x - lane // P) * quarter, SL))
+                phase = orders * (t * P + lane % P) - (lane // P) * quarter
+                upright.append(cos_of(phase, SL))
+                swapped = pltpu.roll(upright[t], P, 1)
+                turned.append(jnp.where(left, -swapped, swapped))
+                for x, value in ((0, upright[t]), (1, turned[t])):
+                    hi, lo = split(value)
                     alpha_hi[h, x * M : (x + 1) * M, at] = hi
                     alpha_lo[h, x * M : (x + 1) * M, at] = lo
-                phase = orders * ((t % 2) * M + lane)
-                hi, lo = split(cos_of(phase + (t // 2) * quarter, SL))
+            for t in range(4):
+                at = slice(t * M, (t + 1) * M)
+                one = t % 2 * 2
+                if t < 2:
+                    value = jnp.where(left, upright[one], turned[one + 1])
+                else:
+                    value = jnp.where(left, turned[one], -upright[one + 1])
+                hi, lo = split(value)
                 gamma_hi[h * M : (h + 1) * M, at] = hi
                 gamma_lo[h * M : (h + 1) * M, at] = lo
 
@@ -223,56 +247,55 @@
             device_id={"degree": 1 - deg}, device_id_type=MESH,
         )
 
-    def compute(h, arrivals):
+    def unit(h, start, size, last):
         mag_p = jnp.abs(col[pl.ds(pl.multiple_of(me * P, P), P), :])
         mag_m = jnp.abs(row_ref[h] - SL // 2)
         most = jnp.maximum(mag_p, jnp.broadcast_to(mag_m, (P, M)))
         most = jnp.concatenate([most, most], axis=0)
-
-        def chunk(c, carry):
-            arrivals(c)
-            for i in range(per):
-                step = c * per + i
-                b0, b1 = sbuf[2 * h, step], sbuf[2 * h + 1, step]
-                low = jnp.concatenate([b0[:, :P], b1[:, :P]], axis=1)
-                high = jnp.concatenate([b0[:, P:], b1[:, P:]], axis=1)
-                for part, scene in ((0, low), (1, high)):
-                    l = step + part * HL
-                    grip = g32[pl.ds(l, K, stride=L), :].astype(BF16)
-                    value = lax.dot_general(grip, scene, dims, preferred_element_type=F32)
-                    value = jnp.where(most <= deg * L + l, value, F32(0.0))
-                    prod[part, i] = value.astype(BF16)
-            w_copy(h, c).wait()
-
-            def rows(blk, carry):
-                at = pl.multiple_of(blk * ROWS, ROWS)
-
-                def degree_step(i, acc):
-                    acc = list(acc)
-                    for part in range(2):
-                        pr = prod[part, i, pl.ds(at, ROWS), :].astype(F32)
-                        pi = prod[part, i, pl.ds(at + P, ROWS), :].astype(F32)
-                        for b in range(NBETA):
-                            w = wbuf[h, part, c * per + i, b, pl.ds(at, ROWS), :].astype(F32)
-                            acc[2 * b] += pr * w
-                            acc[2 * b + 1] += pi * w
-                    return tuple(acc)
-
-                acc = tuple(accbuf[h, blk, n // 2, n % 2] for n in range(2 * NBETA))
-                acc = lax.fori_loop(0, per, degree_step, acc, unroll=2)
-                for n in range(2 * NBETA):
-                    accbuf[h, blk, n // 2, n % 2] = acc[n]
-
-                @pl.when(c == CHUNKS - 1)
-                def _():
-                    rs_send[h, blk] = accbuf[h, blk, pl.ds((1 - deg) * BO, BO)].astype(BF16)
-                    r_copy(h, blk).start()
-
-                return carry
-
-            return lax.fori_loop(0, blocks, rows, carry)
-
-        lax.fori_loop(0, CHUNKS, chunk, 0)
+        for i in range(size):
+            step = start + i
+            b0, b1 = sbuf[2 * h, step], sbuf[2 * h + 1, step]
+            low = jnp.concatenate([b0[:, :P], b1[:, :P]], axis=1)
+            high = jnp.concatenate([b0[:, P:], b1[:, P:]], axis=1)
+            for part, scene in ((0, low), (1, high)):
+                l = step + part * HL
+                grip = g32[pl.ds(l, K, stride=L), :].astype(BF16)
+                value = lax.dot_general(grip, scene, dims, preferred_element_type=F32)
+                value = jnp.where(most <= deg * L + l, value, F32(0.0))
+                prod[part, i] = value.astype(BF16)
+
+        def rows(blk, carry):
+            at = pl.multiple_of(blk * ROWS, ROWS)
+
+            def degree_step(i, acc):
+                acc = list(acc)
+                for part in range(2):
+                    pr = prod[part, i, pl.ds(at, ROWS), :].astype(F32)
+                    pi = prod[part, i, pl.ds(at + P, ROWS), :].astype(F32)
+                    for b in range(NBETA):
+                        w = wbuf[h, part, start + i, b, pl.ds(at, ROWS), :].astype(F32)
+                        acc[2 * b] += pr * w
+                        acc[2 * b + 1] += pi * w
+                return tuple(acc)
+
+            acc = tuple(accbuf[h, blk, n // 2, n % 2] for n in range(2 * NBETA))
+            acc = lax.fori_loop(0, size, degree_step, acc, unroll=2)
+            for n in range(2 * NBETA):
+                accbuf[h, blk, n // 2, n % 2] = acc[n]
+
+            def scatter():
+                rs_send[h, blk] = accbuf[h, blk, pl.ds((1 - deg) * BO, BO)].astype(BF16)
+                r_copy(h, blk).start()
+
+            if isinstance(last, bool):
+                if last:
+                    scatter()
+            else:
+                pl.when(last)(scatter)
+
+            return carry
+
+        lax.fori_loop(0, blocks, rows, 0)
 
     def alpha(h, blk):
         r_copy(h, blk).wait_recv()
@@ -294,7 +317,7 @@
     def wait_block(block, c):
         hop(block, c, me // 3).wait_recv()
 
-    def arrivals_first(c):
+    def collect(c):
         wait_block(near, c)
 
         @pl.when(middle)
@@ -303,37 +326,56 @@
             wait_block(other, c)
             hop(other, c, 1 - across).start()
 
-    def arrivals_second(c):
+    def relay(c):
         @pl.when(middle)
         def _():
             wait_block(beyond, c)
             hop(beyond, c, 1 - across).start()
 
+    def wait_second(i):
         @pl.when(jnp.logical_not(middle))
         def _():
-            wait_block(second * 2, c)
-            wait_block(second * 2 + 1, c)
-
-    select(0)
-    pl.semaphore_wait(barrier, 4)
-    send_own(0)
-    select(1)
-    send_own(1)
-    w_copy(first, 0).start()
-    for c in range(2, CHUNKS):
-        arrivals_first(c - 2)
-        select(c)
-        send_own(c)
-        w_copy(first, c - 1).start()
-    w_copy(first, CHUNKS - 1).start()
-    for c in range(CHUNKS):
-        w_copy(second, c).start()
-    arrivals_first(CHUNKS - 2)
-    prepare()
-    arrivals_first(CHUNKS - 1)
-    tables()
-    compute(first, lambda c: None)
-    compute(second, arrivals_second)
+            wait_block(second * 2, i)
+            wait_block(second * 2 + 1, i)
+
+    def own(i):
+        select(i)
+        if i == 0:
+            pl.semaphore_wait(barrier, 4)
+        send_own(i)
+
+    def fetch_first(c):
+        w_copy(first, c).start()
+
+    def fetch_second():
+        for c in range(CHUNKS):
+            w_copy(second, c).start()
+
+    def unit_first(c):
+        w_copy(first, c).wait()
+        unit(first, c * per, per, c == CHUNKS - 1)
+
+    def unit_second(n):
+        start, size, pieces = UNITS[n]
+        for i in pieces:
+            wait_second(i)
+        if start % per == 0:
+            w_copy(second, start // per).wait()
+        unit(second, start, size, n == len(UNITS) - 1)
+
+    def alpha_first():
+        for blk in range(blocks):
+            halfacc[blk] = alpha(first, blk)
+
+    def stage(c):
+        c_copy(c).start()
+
+    acts = {
+        "s": own, "c": collect, "r": relay, "f": fetch_first, "x": fetch_second, "p": prepare,
+        "t": tables, "u": unit_first, "v": unit_second, "a": alpha_first, "k": stage,
+    }
+    for item in sum((part.split() for part in PLAN), []):
+        acts[item[0]](*[int(item[1:])] if item[1:] else [])
 
     def x_copy(target, source, blk, off):
         return pltpu.make_async_remote_copy(
@@ -343,13 +385,12 @@
         )
 
     for blk in range(blocks):
-        halfacc[blk] = alpha(first, blk)
-    for blk in range(blocks):
         value = (halfacc[blk] + alpha(second, blk)).astype(BF16)
         for t in range(4):
             a_send[t, blk] = value[:, t * M : (t + 1) * M]
-        for off in (2, 1, 3):
-            x_copy((me + off) % 4, me, blk, off).start()
+        for off in (3, 2, 1):
+            far = jnp.where(me < 2, (me + off) % 4, (me - off + 4) % 4)
+            x_copy(far, me, blk, (far - me + 4) % 4).start()
         a_recv[me, blk] = a_send[me, blk]
 
     for blk in range(blocks):
@@ -373,7 +414,7 @@
             )
     out_ref[0] = score.reshape(BO, P, SL)
 
-    for c in range(CHUNKS):
+    for c in range(len(PIECES)):
         @pl.when(me < 3)
         def _():
             hop(me, c, 0).wait_send()
@@ -414,8 +455,7 @@
         scratch_shapes=[
             pltpu.VMEM((2, 2, L // 2, NBETA, P, M), BF16),
             *[
-                pltpu.VMEM((K, 2, L // 2 // CHUNKS, cand // GROUP, GROUP, P), BF16)
-                for _ in range(CHUNKS)
+                pltpu.VMEM((K, 2, size, cand // GROUP, GROUP, P), BF16) for size in PIECES
             ],
             pltpu.VMEM((2, K // 2, L, P), BF16),
             pltpu.VMEM((2, 1, M), jnp.int32),
@@ -434,10 +474,10 @@
             pltpu.VMEM((K * L, 2 * P), F32),
             pltpu.VMEM((SL, M), jnp.int32),
             pltpu.SemaphoreType.DMA((2,)),
-            pltpu.SemaphoreType.DMA((CHUNKS,)),
+            pltpu.SemaphoreType.DMA((len(PIECES),)),
             pltpu.SemaphoreType.DMA((2, CHUNKS)),
-            pltpu.SemaphoreType.DMA((2, 4, CHUNKS)),
-            pltpu.SemaphoreType.DMA((4, CHUNKS)),
+            pltpu.SemaphoreType.DMA((2, 4, len(PIECES))),
+            pltpu.SemaphoreType.DMA((4, len(PIECES))),
             pltpu.SemaphoreType.DMA((2, NB)),
             pltpu.SemaphoreType.DMA((2, NB)),
             pltpu.SemaphoreType.DMA((4, NB)),
@@ -449,8 +489,8 @@
     )(
         tall,
         site_ids,
-        gripper_coeffs,
-        order_table.reshape(2, 1, M),
+        pltpu.with_memory_space_constraint(gripper_coeffs, pltpu.HBM),
+        pltpu.with_memory_space_constraint(order_table.reshape(2, 1, M), pltpu.HBM),
         wigner.reshape(2, L // 2, NBETA, P, SL),
     )
 

time: 46.2 us -> 36.8 us (0.80)
  Pallas kernels: 42.9 us -> 35.2 us
  local copies, waits for them, and re-layouts: 2.42 us -> 0.71 us
    pallas_call x1, Pallas kernels: 42.9 us -> 35.2 us  [fused_shards(): pl.pallas_call(fused_kernel, out_shape=jax.ShapeDtypeStruct((1, BO, P, SL...]
    unnamed x5 -> x1, local copies, waits for them, and re-layouts: 2.42 us -> 0.71 us
where the time goes in v3:
time: 36.8 us; the launch traced here: 36.6 us
  Pallas kernels  35.2 us (96%)
  local copies, waits for them, and re-layouts  0.71 us (2%)
  between operations  0.66 us (2%)
    pallas_call x1, Pallas kernels, fused_shards(): pl.pallas_call(fused_kernel, out_shape=jax.ShapeDtypeStruct((1, BO, P, SL...  35.2 us

profile of v3, /device:TPU:0, one launch (start us, length us, event | category | flops | bytes accessed | tf_op | source)
XLA Modules:
  0.0 36.6 jit_solution(1354416422146742991)
XLA Ops:
  0.7 35.2 %shard_map.55 = f32[1,4,64,256]{3,2,1,0:T(8,128)S(1)} custom-call(bf16[32,2,32,4,8,64]{5,4,3,2,1,0:T(8,128)(2,1)} %bitcast.5, s32[1]{0:T(128)S(6)} %copy.7.site_ref, bf16[2,16,64,64]{3,2,1,0:T(8,128)(2,1)} %g_hbm.1, s32[2,1,128]{2,1,0:T(1,128)} %bitcast.7, bf16[2,32,8,64,256]{4,3,2,1,0:T(8,128)(2,1)} %bitcast.6), custom_call_target="tpu_custom_call" | custom-call | tf_op jit(solution)/shard_map/pallas_call | solution.py:450
  35.9 0.7 %copy.8 = f32[1,4,64,256]{3,2,1,0:T(8,128)} copy(f32[1,4,64,256]{3,2,1,0:T(8,128)S(1)} %shard_map.55) | data formatting | bytes 524288

commit v4 on v3

--- a/solution.py
+++ b/solution.py
@@ -111,14 +111,14 @@
 
 
 def fused_kernel(
-    scene_ref, site_ref, g_hbm, row_hbm, w_ref, out_ref, wbuf, *scratch
+    scene_ref, site_ref, g_hbm, row_hbm, w_ref, out_ref, last_ref, wbuf, *scratch
 ):
     cands, scratch = scratch[: len(PIECES)], scratch[len(PIECES) :]
-    fused_body(scene_ref, site_ref, g_hbm, row_hbm, w_ref, out_ref, wbuf, cands, *scratch)
+    fused_body(scene_ref, site_ref, g_hbm, row_hbm, w_ref, out_ref, last_ref, wbuf, cands, *scratch)
 
 
 def fused_body(
-    scene_ref, site_ref, g_hbm, row_hbm, w_ref, out_ref, wbuf, cands,
+    scene_ref, site_ref, g_hbm, row_hbm, w_ref, out_ref, last_ref, wbuf, cands,
     g_ref, row_ref, sbuf, prod, accbuf, rs_send, rs_recv, a_send, a_recv, halfacc,
     alpha_hi, alpha_lo, gamma_hi, gamma_lo, g32, col,
     in_sem, c_sem, w_sem, s_send_sem, s_recv_sem, r_send_sem, r_recv_sem, x_send_sem, x_recv_sem,
@@ -264,7 +264,7 @@
                 value = jnp.where(most <= deg * L + l, value, F32(0.0))
                 prod[part, i] = value.astype(BF16)
 
-        def rows(blk, carry):
+        def rows(blk, low, count):
             at = pl.multiple_of(blk * ROWS, ROWS)
 
             def degree_step(i, acc):
@@ -272,30 +272,36 @@
                 for part in range(2):
                     pr = prod[part, i, pl.ds(at, ROWS), :].astype(F32)
                     pi = prod[part, i, pl.ds(at + P, ROWS), :].astype(F32)
-                    for b in range(NBETA):
-                        w = wbuf[h, part, start + i, b, pl.ds(at, ROWS), :].astype(F32)
+                    for b in range(count):
+                        w = wbuf[h, part, start + i, low + b, pl.ds(at, ROWS), :].astype(F32)
                         acc[2 * b] += pr * w
                         acc[2 * b + 1] += pi * w
                 return tuple(acc)
 
-            acc = tuple(accbuf[h, blk, n // 2, n % 2] for n in range(2 * NBETA))
+            acc = tuple(accbuf[h, blk, low + n // 2, n % 2] for n in range(2 * count))
             acc = lax.fori_loop(0, size, degree_step, acc, unroll=2)
-            for n in range(2 * NBETA):
-                accbuf[h, blk, n // 2, n % 2] = acc[n]
-
-            def scatter():
-                rs_send[h, blk] = accbuf[h, blk, pl.ds((1 - deg) * BO, BO)].astype(BF16)
-                r_copy(h, blk).start()
-
-            if isinstance(last, bool):
-                if last:
-                    scatter()
-            else:
-                pl.when(last)(scatter)
-
+            for n in range(2 * count):
+                accbuf[h, blk, low + n // 2, n % 2] = acc[n]
+
+        def whole(blk, carry):
+            rows(blk, 0, NBETA)
             return carry
 
-        lax.fori_loop(0, blocks, rows, 0)
+        def given(blk, carry):
+            rows(blk, (1 - deg) * BO, BO)
+            rs_send[h, blk] = accbuf[h, blk, pl.ds((1 - deg) * BO, BO)].astype(BF16)
+            r_copy(h, blk).start()
+            return carry
+
+        def kept(blk, carry):
+            rows(blk, deg * BO, BO)
+            return carry
+
+        if last:
+            lax.fori_loop(0, blocks, given, 0)
+            lax.fori_loop(0, blocks, kept, 0)
+        else:
+            lax.fori_loop(0, blocks, whole, 0)
 
     def alpha(h, blk):
         r_copy(h, blk).wait_recv()
@@ -393,26 +399,39 @@
             x_copy(far, me, blk, (far - me + 4) % 4).start()
         a_recv[me, blk] = a_send[me, blk]
 
-    for blk in range(blocks):
-        for off in (1, 3, 2):
-            source = (me - off + 4) % 4
-            x_copy(source, source, blk, off).wait_recv()
-
-    score = jnp.zeros((BO * P, SL), F32)
-    got = [
-        jnp.concatenate(
-            [a_recv[z, blk, b * ROWS : (b + 1) * ROWS, :] for z in range(4) for blk in range(blocks)],
+    def gamma(source):
+        rows = pl.ds(pl.multiple_of(source * P, P), P)
+        got = [
+            jnp.concatenate(
+                [a_recv[source, blk, b * ROWS : (b + 1) * ROWS, :] for blk in range(blocks)], axis=0
+            )
+            for b in range(BO)
+        ]
+        parts = [
+            jnp.concatenate([piece[:, x * P : (x + 1) * P] for piece in got], axis=1)
+            for x in range(2)
+        ]
+        left = jnp.concatenate(parts + parts, axis=0)
+        right = jnp.concatenate(
+            [
+                table[rows, x * SL : (x + 1) * SL]
+                for table in (gamma_hi, gamma_lo)
+                for x in range(2)
+            ],
             axis=0,
         )
-        for b in range(BO)
-    ]
-    for x in range(2):
-        left = jnp.concatenate([piece[:, x * P : (x + 1) * P] for piece in got], axis=1)
-        for table in (gamma_hi, gamma_lo):
-            score += lax.dot_general(
-                left, table[:, x * SL : (x + 1) * SL], dims, preferred_element_type=F32
-            )
-    out_ref[0] = score.reshape(BO, P, SL)
+        score = lax.dot_general(left, right, dims, preferred_element_type=F32)
+        return score.reshape(BO, P, SL)
+
+    out_ref[0] = gamma(me)
+    for off in (1, 2, 3):
+        source = jnp.where(me < 2, (me + off) % 4, (me - off + 4) % 4)
+        for blk in range(blocks):
+            x_copy(source, source, blk, (me - source + 4) % 4).wait_recv()
+        if off < 3:
+            out_ref[0] += gamma(source)
+        else:
+            last_ref[0] = gamma(source)
 
     for c in range(len(PIECES)):
         @pl.when(me < 3)
@@ -447,11 +466,11 @@
     tall = tall.reshape(K, 2, L // 2, cand // GROUP, GROUP, P)
     vmem = pl.BlockSpec(memory_space=pltpu.VMEM)
     hbm = pl.BlockSpec(memory_space=pltpu.HBM)
-    return pl.pallas_call(
+    score, last = pl.pallas_call(
         fused_kernel,
-        out_shape=jax.ShapeDtypeStruct((1, BO, P, SL), F32),
+        out_shape=[jax.ShapeDtypeStruct((1, BO, P, SL), F32)] * 2,
         in_specs=[hbm, pl.BlockSpec(memory_space=pltpu.SMEM), hbm, hbm, hbm],
-        out_specs=vmem,
+        out_specs=[vmem, vmem],
         scratch_shapes=[
             pltpu.VMEM((2, 2, L // 2, NBETA, P, M), BF16),
             *[
@@ -493,6 +512,7 @@
         pltpu.with_memory_space_constraint(order_table.reshape(2, 1, M), pltpu.HBM),
         wigner.reshape(2, L // 2, NBETA, P, SL),
     )
+    return score + last
 
 
 def solution(mesh):

time: 36.8 us -> 36.6 us (level)
  other arithmetic: 0 us -> 0.74 us
  local copies, waits for them, and re-layouts: 0.71 us -> 0 us
    add x0 -> x1, other arithmetic: none -> 0.74 us  [fused_shards(): return score + last]
    unnamed x1 -> x0, local copies, waits for them, and re-layouts: 0.71 us -> none
where the time goes in v4:
time: 36.6 us; the launch traced here: 36.4 us
  Pallas kernels  35 us (96%)
  other arithmetic  0.74 us (2%)
  between operations  0.66 us (2%)
    pallas_call x1, Pallas kernels, fused_shards(): pl.pallas_call(fused_kernel, out_shape=[jax.ShapeDtypeStruct((1, BO, P, S...  35 us
    add x1, other arithmetic, fused_shards(): return score + last  0.74 us

profile of v4, /device:TPU:0, one launch (start us, length us, event | category | flops | bytes accessed | tf_op | source)
XLA Modules:
  0.0 36.4 jit_solution(2676306864069558746)
XLA Ops:
  0.7 35.0 %shard_map.55 = (f32[1,4,64,256]{3,2,1,0:T(8,128)S(1)}, f32[1,4,64,256]{3,2,1,0:T(8,128)S(1)}) custom-call(bf16[32,2,32,4,8,64]{5,4,3,2,1,0:T(8,128)(2,1)} %bitcast.5, s32[1]{0:T(128)S(6)} %copy.6.site_ref, bf16[2,16,64,64]{3,2,1,0:T(8,128)(2,1)} %g_hbm.1, s32[2,1,128]{2,1,0:T(1,128)} %bitcast.7, bf16[2,32,8,64,256]{4,3,2,1,0:T(8,128)(2,1)} %bitcast.6), custom_call_target="tpu_custom_call" | custom-call | tf_op jit(solution)/shard_map/pallas_call | solution.py:469
  35.7 0.7 %add.3 = f32[1,4,64,256]{3,2,1,0:T(8,128)} add(f32[1,4,64,256]{3,2,1,0:T(8,128)S(1)} %get-tuple-element.7, f32[1,4,64,256]{3,2,1,0:T(8,128)S(1)} %get-tuple-element.8) | non-fusion elementwise | flops 65536 | bytes 786432 | tf_op jit(solution)/shard_map/add | solution.py:515

commit v5 on v4

--- a/solution.py
+++ b/solution.py
@@ -84,8 +84,8 @@
     "s0 s1 s2 s3",
     "f0 f1 f2 f3",
     "x c0 p c1",
-    "u0 c2 u1 c3",
-    "r0 u2 r1 u3",
+    "u0 c2 u1 r0",
+    "c3 u2 r1 u3",
     "r2 t r3 v0",
     "v1 v2 v3 a",
 )
@@ -390,6 +390,21 @@
             device_id={"order": target}, device_id_type=MESH,
         )
 
+    for c in range(len(PIECES)):
+        @pl.when(me < 3)
+        def _():
+            hop(me, c, 0).wait_send()
+
+        @pl.when(me > 0)
+        def _():
+            hop(me, c, 1).wait_send()
+
+        @pl.when(middle)
+        def _():
+            hop(near, c, across).wait_send()
+            hop(other, c, 1 - across).wait_send()
+            hop(beyond, c, 1 - across).wait_send()
+
     for blk in range(blocks):
         value = (halfacc[blk] + alpha(second, blk)).astype(BF16)
         for t in range(4):
@@ -426,33 +441,18 @@
     out_ref[0] = gamma(me)
     for off in (1, 2, 3):
         source = jnp.where(me < 2, (me + off) % 4, (me - off + 4) % 4)
+        if off == 3:
+            for blk in range(blocks):
+                for away in (1, 2, 3):
+                    x_copy((me + away) % 4, me, blk, away).wait_send()
+                r_copy(first, blk).wait_send()
+                r_copy(second, blk).wait_send()
         for blk in range(blocks):
             x_copy(source, source, blk, (me - source + 4) % 4).wait_recv()
         if off < 3:
             out_ref[0] += gamma(source)
         else:
             last_ref[0] = gamma(source)
-
-    for c in range(len(PIECES)):
-        @pl.when(me < 3)
-        def _():
-            hop(me, c, 0).wait_send()
-
-        @pl.when(me > 0)
-        def _():
-            hop(me, c, 1).wait_send()
-
-        @pl.when(middle)
-        def _():
-            hop(near, c, across).wait_send()
-            hop(other, c, 1 - across).wait_send()
-            hop(beyond, c, 1 - across).wait_send()
-
-    for blk in range(blocks):
-        for off in (1, 2, 3):
-            x_copy((me + off) % 4, me, blk, off).wait_send()
-        r_copy(first, blk).wait_send()
-        r_copy(second, blk).wait_send()
 
 
 def fused_shards(scene_coeffs, site_ids, gripper_coeffs, order_table, wigner):

time: 36.6 us -> 36.5 us (level)
  no operation moved by 1% of the time
where the time goes in v5:
time: 36.5 us; the launch traced here: 36.3 us
  Pallas kernels  35 us (96%)
  other arithmetic  0.74 us (2%)
  between operations  0.66 us (2%)
    pallas_call x1, Pallas kernels, fused_shards(): pl.pallas_call(fused_kernel, out_shape=[jax.ShapeDtypeStruct((1, BO, P, S...  35 us
    add x1, other arithmetic, fused_shards(): return score + last  0.74 us

profile of v5, /device:TPU:0, one launch (start us, length us, event | category | flops | bytes accessed | tf_op | source)
XLA Modules:
  0.0 36.3 jit_solution(18146987208146970918)
XLA Ops:
  0.7 35.0 %shard_map.55 = (f32[1,4,64,256]{3,2,1,0:T(8,128)S(1)}, f32[1,4,64,256]{3,2,1,0:T(8,128)S(1)}) custom-call(bf16[32,2,32,4,8,64]{5,4,3,2,1,0:T(8,128)(2,1)} %bitcast.5, s32[1]{0:T(128)S(6)} %copy.6.site_ref, bf16[2,16,64,64]{3,2,1,0:T(8,128)(2,1)} %g_hbm.1, s32[2,1,128]{2,1,0:T(1,128)} %bitcast.7, bf16[2,32,8,64,256]{4,3,2,1,0:T(8,128)(2,1)} %bitcast.6), custom_call_target="tpu_custom_call" | custom-call | tf_op jit(solution)/shard_map/pallas_call | solution.py:469
  35.6 0.7 %add.3 = f32[1,4,64,256]{3,2,1,0:T(8,128)} add(f32[1,4,64,256]{3,2,1,0:T(8,128)S(1)} %get-tuple-element.7, f32[1,4,64,256]{3,2,1,0:T(8,128)S(1)} %get-tuple-element.8) | non-fusion elementwise | flops 65536 | bytes 786432 | tf_op jit(solution)/shard_map/add | solution.py:515

commit v6 on v5

--- a/solution.py
+++ b/solution.py
@@ -150,6 +150,11 @@
             scene_ref.at[:, :, pl.ds(starts[c], PIECES[c])], cands[c], c_sem.at[c]
         )
 
+    barrier = pltpu.get_barrier_semaphore()
+    for off in (1, 2, 3):
+        pl.semaphore_signal(barrier, 1, device_id={"order": (me + off) % 4}, device_id_type=MESH)
+    pl.semaphore_signal(barrier, 1, device_id={"degree": 1 - deg}, device_id_type=MESH)
+
     c_copy(0).start()
     g_copy = pltpu.make_async_copy(g_hbm, g_ref, in_sem.at[0])
     row_copy = pltpu.make_async_copy(row_hbm, row_ref, in_sem.at[1])
@@ -157,11 +162,6 @@
     g_copy.start()
     for c in range(1, STAGED):
         c_copy(c).start()
-
-    barrier = pltpu.get_barrier_semaphore()
-    for off in (1, 2, 3):
-        pl.semaphore_signal(barrier, 1, device_id={"order": (me + off) % 4}, device_id_type=MESH)
-    pl.semaphore_signal(barrier, 1, device_id={"degree": 1 - deg}, device_id_type=MESH)
 
     site = site_ref[0]
     pick_row = lax.broadcasted_iota(jnp.int32, (K, K * GROUP), 0)
@@ -279,7 +279,7 @@
                 return tuple(acc)
 
             acc = tuple(accbuf[h, blk, low + n // 2, n % 2] for n in range(2 * count))
-            acc = lax.fori_loop(0, size, degree_step, acc, unroll=2)
+            acc = lax.fori_loop(0, size, degree_step, acc, unroll=4)
             for n in range(2 * count):
                 accbuf[h, blk, low + n // 2, n % 2] = acc[n]
 

time: 36.5 us -> 36.5 us (level)
  no operation moved by 1% of the time
where the time goes in v6:
time: 36.5 us; the launch traced here: 36.3 us
  Pallas kernels  34.9 us (96%)
  other arithmetic  0.74 us (2%)
  between operations  0.66 us (2%)
    pallas_call x1, Pallas kernels, fused_shards(): pl.pallas_call(fused_kernel, out_shape=[jax.ShapeDtypeStruct((1, BO, P, S...  34.9 us
    add x1, other arithmetic, fused_shards(): return score + last  0.74 us

profile of v6, /device:TPU:0, one launch (start us, length us, event | category | flops | bytes accessed | tf_op | source)
XLA Modules:
  0.0 36.3 jit_solution(1177789904547935455)
XLA Ops:
  0.7 34.9 %shard_map.55 = (f32[1,4,64,256]{3,2,1,0:T(8,128)S(1)}, f32[1,4,64,256]{3,2,1,0:T(8,128)S(1)}) custom-call(bf16[32,2,32,4,8,64]{5,4,3,2,1,0:T(8,128)(2,1)} %bitcast.5, s32[1]{0:T(128)S(6)} %copy.6.site_ref, bf16[2,16,64,64]{3,2,1,0:T(8,128)(2,1)} %g_hbm.1, s32[2,1,128]{2,1,0:T(1,128)} %bitcast.7, bf16[2,32,8,64,256]{4,3,2,1,0:T(8,128)(2,1)} %bitcast.6), custom_call_target="tpu_custom_call" | custom-call | tf_op jit(solution)/shard_map/pallas_call | solution.py:469
  35.6 0.7 %add.3 = f32[1,4,64,256]{3,2,1,0:T(8,128)} add(f32[1,4,64,256]{3,2,1,0:T(8,128)S(1)} %get-tuple-element.7, f32[1,4,64,256]{3,2,1,0:T(8,128)S(1)} %get-tuple-element.8) | non-fusion elementwise | flops 65536 | bytes 786432 | tf_op jit(solution)/shard_map/add | solution.py:515
